TPU v7x, 128 devices: a whole 4x4x4 slice. The times are simulated.
128 devices in a mesh: dp: 8 (over x, core), tp: 16 (over y, z).
Axes of the slice: x: 4, y: 4, z: 4, core: 2. Of those that a mesh axis runs over, the one named last changes fastest.
Arguments:
- queries: bfloat16 [1024, 128, 576], P(('dp', 'tp')), may hold values from -10 to 10
- new_latent: bfloat16 [1024, 576], P(('dp', 'tp')), may hold values from -6 to 6
- resident: bfloat16 [768, 256, 576], P(('dp', 'tp')), may hold values from -6 to 6
- leaving: bfloat16 [256, 2, 256, 576], P(('dp', 'tp')), may hold values from -6 to 6
- res_len: int32 [768], P(('dp', 'tp')), may hold values from 1 to 256, as said below
- leave_len: int32 [128, 2], replicated, may hold values from 1 to 256, as said below
- mig_dest: int32 [128, 2], replicated, may hold values from 0 to 15, as said below
- stream: bfloat16 [1024, 7168], P(('dp', 'tp')), may hold values from -6 to 6
- dense_gain: float32 [7168], replicated, may hold values from 0.1 to 1.9
- w_gate: bfloat16 [7168, 18432], P('dp', 'tp'), may hold values from -0.0625 to 0.0625
- w_up: bfloat16 [7168, 18432], P('dp', 'tp'), may hold values from -0.0625 to 0.0625
- w_down: bfloat16 [18432, 7168], P('tp', 'dp'), may hold values from -0.046875 to 0.046875
- moe_gain: float32 [7168], replicated, may hold values from 0.1 to 1.9
- expert_gate: bfloat16 [16, 7168, 2048], P('tp', None, 'dp'), may hold values from -0.0625 to 0.0625
- expert_up: bfloat16 [16, 7168, 2048], P('tp', None, 'dp'), may hold values from -0.0625 to 0.0625
- expert_down: bfloat16 [16, 2048, 7168], P('tp', 'dp'), may hold values from -0.125 to 0.125
- expert_ids: int32 [1024, 8], P(('dp', 'tp')), may hold values from 0 to 15, all different within a row; in each aligned block of 8 rows (0 to 7, 8 to 15, ...) at most 5 rows name the same one
- gate_scores: float32 [1024, 8], P(('dp', 'tp')), may hold values from 0.05 to 1
Outputs:
- context: bfloat16 [1024, 128, 512], P(('dp', 'tp'))
- arrived: bfloat16 [256, 2, 256, 576], P(('dp', 'tp'))
- stream_out: bfloat16 [1024, 7168], P(('dp', 'tp'))
Inputs may be any that keep to these rules, and one draw needn't show every extreme that they name: `mig_dest`: each device sends its 2 leaving requests to 2 different other devices of its dp index, and every device receives exactly 2 requests. `res_len`: some request holds all 256 positions. `leave_len`: some request holds all 256 positions. `expert_ids`: among the 8 rows of one device no expert is chosen by more than 5 rows, a bound that some block reaches; a row names 8 different experts.
All inputs are finite; a program needn't handle non-finite values.
Results may differ from a plain program's by a relative error of at most 0.023.
Values may be sent and summed in bfloat16 or wider, within the bound.
A program may use at most 128 MiB of HBM per device.

v0:
```python
import jax
import jax.numpy as jnp
from jax import lax
from jax.sharding import PartitionSpec as P

VDIM = 512
QKD = 192
EPS = 1e-06
ROUTE_SCALE = 2.5


def rms_scale(rows, gain):
    values = rows.astype(jnp.float32)
    mean_square = jnp.mean(values * values, axis=-1, keepdims=True)
    return (values * lax.rsqrt(mean_square + EPS) * gain).astype(jnp.bfloat16)


def attend(queries, keys, lengths, newest):
    scale = QKD ** (-0.5)
    scores = jnp.einsum("rhl,rcl->rhc", queries, keys, preferred_element_type=jnp.float32) * scale
    positions = jnp.arange(keys.shape[1])
    valid = positions[None, None, :] < lengths[:, None, None]
    masked = jnp.where(valid, scores, -1e30)
    own_score = (
        jnp.einsum("rhl,rl->rh", queries, newest, preferred_element_type=jnp.float32) * scale
    )
    top = jnp.maximum(jnp.max(masked, axis=-1), own_score)
    expo = jnp.where(valid, jnp.exp(masked - top[..., None]), 0.0)
    own_expo = jnp.exp(own_score - top)
    total = jnp.sum(expo, axis=-1) + own_expo
    weights = (expo / total[..., None]).astype(jnp.bfloat16)
    own_weight = (own_expo / total).astype(jnp.bfloat16)
    context = jnp.einsum(
        "rhc,rcv->rhv", weights, keys[:, :, :VDIM], preferred_element_type=jnp.float32
    )
    context = context + own_weight.astype(jnp.float32)[..., None] * newest[:, None, :VDIM].astype(
        jnp.float32
    )
    return context.astype(jnp.bfloat16)


def on_device(
    queries,
    new_latent,
    resident,
    leaving,
    res_len,
    leave_len,
    mig_dest,
    stream,
    dense_gain,
    w_gate,
    w_up,
    w_down,
    moe_gain,
    expert_gate,
    expert_up,
    expert_down,
    expert_ids,
    gate_scores,
):
    tp_count = lax.axis_size("tp")
    dp_count = lax.axis_size("dp")
    tp_rank = lax.axis_index("tp")
    dp_rank = lax.axis_index("dp")
    moving = leaving.shape[0]
    device = dp_rank * tp_count + tp_rank
    peers = jnp.arange(tp_count)
    own_dest = lax.dynamic_index_in_dim(mig_dest, device, 0, keepdims=False)
    outgoing = jnp.zeros((tp_count,) + leaving.shape[1:], jnp.bfloat16)
    for slot in range(moving):
        outgoing = jnp.where(
            (peers == own_dest[slot])[:, None, None, None], leaving[slot][None], outgoing
        )
    incoming = lax.all_to_all(outgoing, "tp", split_axis=0, concat_axis=0, tiled=True)
    group_dest = lax.dynamic_slice_in_dim(mig_dest, dp_rank * tp_count, tp_count, 0)
    group_len = lax.dynamic_slice_in_dim(leave_len, dp_rank * tp_count, tp_count, 0)
    match = group_dest == tp_rank
    is_source = jnp.any(match, axis=1)
    which = jnp.sum(jnp.where(match, jnp.arange(moving)[None, :], 0), axis=1)
    order = jnp.cumsum(is_source.astype(jnp.int32)) - 1
    arrivals = []
    arrival_len = []
    for arrival in range(moving):
        pick = is_source & (order == arrival)
        source = jnp.sum(jnp.where(pick, peers, 0))
        slot = jnp.sum(jnp.where(pick, which, 0))
        arrivals.append(lax.dynamic_index_in_dim(incoming, source, 0, keepdims=False))
        source_len = lax.dynamic_index_in_dim(group_len, source, 0, keepdims=False)
        arrival_len.append(lax.dynamic_index_in_dim(source_len, slot, 0, keepdims=False))
    arrived = jnp.stack(arrivals, axis=0)
    arrived_len = jnp.stack(arrival_len, axis=0)
    stay = resident.shape[0]
    context_stay = attend(queries[:stay], resident, res_len, new_latent[:stay])
    context_moved = attend(queries[stay:], arrived[:, 0], arrived_len, new_latent[stay:])
    context = jnp.concatenate([context_stay, context_moved], axis=0)
    rows_dev = stream.shape[0]
    width = stream.shape[1]
    normed = rms_scale(stream, dense_gain)
    nearby = lax.all_gather(normed[None], "tp", axis=0, tiled=True)
    gathered = lax.all_to_all(nearby[:, None], "dp", split_axis=3, concat_axis=1, tiled=True)
    features = gathered.reshape(-1, gathered.shape[-1])
    gate_part = jnp.dot(features, w_gate, preferred_element_type=jnp.float32)
    up_part = jnp.dot(features, w_up, preferred_element_type=jnp.float32)
    gate, up = (
        lax.psum(gate_part.astype(jnp.bfloat16), "dp").astype(jnp.float32),
        lax.psum(up_part.astype(jnp.bfloat16), "dp").astype(jnp.float32),
    )
    hidden_all = (jax.nn.silu(gate) * up).astype(jnp.bfloat16)
    block = hidden_all
    ffn_share = lax.psum_scatter(
        jnp.dot(block, w_down, preferred_element_type=jnp.float32).astype(jnp.bfloat16),
        "tp",
        scatter_dimension=0,
        tiled=True,
    ).astype(jnp.float32)
    ffn_rows = lax.all_to_all(
        ffn_share.reshape(dp_count, rows_dev, ffn_share.shape[-1]).astype(jnp.bfloat16),
        "dp",
        split_axis=0,
        concat_axis=2,
        tiled=True,
    ).astype(jnp.float32)
    middle = (stream.astype(jnp.float32) + ffn_rows[0]).astype(jnp.bfloat16)
    mixed = rms_scale(middle, moe_gain)
    experts = expert_gate.shape[0] * tp_count
    top_count = expert_ids.shape[1]
    capacity = min(rows_dev, rows_dev * top_count // experts + 1)
    hits = (expert_ids[:, :, None] == jnp.arange(experts)[None, None, :]).astype(jnp.int32)
    row_hits = jnp.sum(hits, axis=1)
    before = jnp.cumsum(row_hits, axis=0) - row_hits
    slot_of = jnp.sum(hits * before[:, None, :], axis=2)
    target = expert_ids * capacity + slot_of
    placed = jnp.any(target[:, :, None] == jnp.arange(experts * capacity)[None, None, :], axis=1)
    outgoing_rows = jnp.dot(
        placed.T.astype(jnp.bfloat16), mixed, preferred_element_type=jnp.float32
    )
    outgoing_rows = outgoing_rows.astype(jnp.bfloat16).reshape(experts, capacity, width)
    received = lax.all_to_all(outgoing_rows, "tp", split_axis=0, concat_axis=0, tiled=True)
    pooled = lax.all_gather(received, "dp", axis=0, tiled=True)
    flat = pooled.reshape(-1, width)
    block = flat
    gate = jnp.dot(block, expert_gate[0], preferred_element_type=jnp.float32)
    up = jnp.dot(block, expert_up[0], preferred_element_type=jnp.float32)
    inner = (jax.nn.silu(gate) * up).astype(jnp.bfloat16)
    summed = lax.psum_scatter(
        jnp.dot(inner, expert_down[0], preferred_element_type=jnp.float32).astype(jnp.bfloat16),
        "dp",
        scatter_dimension=0,
        tiled=True,
    )
    results = summed.reshape(received.shape)
    returned = lax.all_to_all(results, "tp", split_axis=0, concat_axis=0, tiled=True)
    flat_back = returned.reshape(experts * capacity, width)
    picked = jnp.take(flat_back, target.reshape(-1), axis=0).reshape(rows_dev, top_count, width)
    shares = gate_scores / jnp.sum(gate_scores, axis=1, keepdims=True) * ROUTE_SCALE
    routed = jnp.einsum("rk,rkd->rd", shares, picked.astype(jnp.float32))
    stream_out = (middle.astype(jnp.float32) + routed).astype(jnp.bfloat16)
    return (context, arrived, stream_out)


def solution(mesh):
    placed = (
        P(("dp", "tp"), None, None),
        P(("dp", "tp"), None),
        P(("dp", "tp"), None, None),
        P(("dp", "tp"), None, None, None),
        P(("dp", "tp")),
        P(),
        P(),
        P(("dp", "tp"), None),
        P(),
        P("dp", "tp"),
        P("dp", "tp"),
        P("tp", "dp"),
        P(),
        P("tp", None, "dp"),
        P("tp", None, "dp"),
        P("tp", "dp", None),
        P(("dp", "tp"), None),
        P(("dp", "tp"), None),
    )
    return jax.shard_map(
        on_device,
        mesh=mesh,
        in_specs=placed,
        out_specs=(
            P(("dp", "tp"), None, None),
            P(("dp", "tp"), None, None, None),
            P(("dp", "tp"), None),
        ),
        check_vma=False,
    )
```

profile of v0, /device:TPU:0, one launch (start us, length us, event | category | flops | bytes accessed | tf_op | source)
XLA Modules:
  0.0 688.6 jit_solution(10923640459823760998)
XLA Ops:
  7.2 1.2 fusion.49
  8.4 1.6 fusion.51
  10.2 47.7 %all-gather.6.cloned.1.call-done = bf16[128,7168]{1,0:T(8,128)(2,1)} async-done(((bf16[8,7168]{1,0:T(8,128)(2,1)}), bf16[128,7168]{1,0:T(8,128)(2,1)}) %all-gather.6.cloned.1.call-update) | async-done | bytes 1835024 | tf_op jit(solution)/shard_map/all_gather | solution.py:100
  57.8 13.7 %copy.81 = bf16[16,1,8,7168]{0,2,1,3:T(8,128)(2,1)} copy(bf16[16,1,8,7168]{3,2,0,1:T(8,128)(2,1)} %bitcast.99) | data formatting | bytes 3670016 | tf_op jit(solution)/shard_map/broadcast_in_dim | solution.py:101
  71.6 17.3 %reshape.231 = bf16[8,2,57344]{2,1,0:T(2,128)(2,1)} reshape(bf16[7168,1,8,16]{3,2,1,0:T(8,128)(2,1)} %bitcast.94) | data formatting | bytes 3670016
  88.8 28.8 %all_to_all.39 = bf16[8,2,57344]{2,1,0:T(2,128)(2,1)} all-to-all(bf16[8,2,57344]{2,1,0:T(2,128)(2,1)} %reshape.231), channel_id=1, replica_groups=mesh['dp'=8,'tp'=16] {'dp'}, dimensions={0} | all-to-all | bytes 3670016 | tf_op jit(solution)/shard_map/all_to_all | solution.py:101
  117.6 12.5 %reshape.232 = bf16[7168,1,8,16]{3,2,1,0:T(8,128)(2,1)} reshape(bf16[8,2,57344]{2,1,0:T(2,128)(2,1)} %all_to_all.39) | data formatting | bytes 3670016
  130.1 13.8 %copy.95 = bf16[16,1,8,8,896]{4,3,2,0,1:T(8,128)(2,1)} copy(bf16[16,1,8,8,896]{0,2,4,3,1:T(8,128)(2,1)} %bitcast.95) | data formatting | bytes 3670016 | tf_op jit(solution)/shard_map/all_to_all | solution.py:101
  143.9 1.8 copy.83
  145.8 4.1 convolution_convert_fusion.2
  149.8 4.1 convolution_convert_fusion.3
  154.0 71.9 %all-reduce.3.cloned.1.call-done = (bf16[1024,1152]{1,0:T(8,128)(2,1)}, bf16[1024,1152]{1,0:T(8,128)(2,1)}) async-done(((bf16[1024,1152]{1,0:T(8,128)(2,1)}, bf16[1024,1152]{1,0:T(8,128)(2,1)}), (bf16[1024,1152]{1,0:T(8,128)(2,1)}, bf16[1024,1152]{1,0:T(8,128)(2,1)})) %all-reduce.3.cloned.1.call-update) | async-done | bytes 4718608 | tf_op jit(solution)/shard_map/psum | solution.py:107
  225.9 7.3 %fusion.12 = bf16[1024,896]{1,0:T(8,128)(2,1)} fusion(bf16[1152,896]{1,0:T(8,128)(2,1)} %param.29, bf16[1024,1152]{1,0:T(8,128)(2,1)} %get-tuple-element.30, bf16[1024,1152]{1,0:T(8,128)(2,1)} %get-tuple-element.31), kind=kOutput, calls=%fused_computation.19 | convolution fusion | flops 2124283904 | bytes 8617984 | tf_op jit(solution)/shard_map/dot_general | solution.py:112
  233.3 0.1 convert_reduce_fusion
  233.4 0.3 select_reduce_fusion
  233.7 75.1 %reduce-scatter.3.cloned.1.call-done = bf16[64,896]{1,0:T(8,128)(2,1)} async-done(((bf16[1024,896]{1,0:T(8,128)(2,1)}), bf16[64,896]{1,0:T(8,128)(2,1)}) %reduce-scatter.3.cloned.1.call-update) | async-done | bytes 114704 | tf_op jit(solution)/shard_map/reduce_scatter | solution.py:111
  308.7 4.3 all-to-all-start.2
  313.0 0.2 all-gather.4.cloned.1.call-start
  313.2 0.1 fusion.65
  313.3 5.6 all-to-all-done.2
  318.9 0.2 fusion.53
  319.1 0.5 convolution_convert_fusion.1
  319.7 0.6 reshape.205
  320.2 29.9 %all_to_all.40 = bf16[16,5,7168]{2,1,0:T(8,128)(2,1)S(1)} all-to-all(bf16[16,5,7168]{2,1,0:T(8,128)(2,1)S(1)} %reshape.205), channel_id=1, replica_groups=mesh['dp'=8,'tp'=16] {'tp'}, dimensions={0} | all-to-all | bytes 2293760 | tf_op jit(solution)/shard_map/all_to_all | solution.py:139
  350.2 1.8 copy.84
  352.0 49.3 %all-gather.4.cloned.1.call-done = bf16[128,5,7168]{2,0,1:T(8,128)(2,1)} async-done(((bf16[16,5,7168]{2,0,1:T(8,128)(2,1)}), bf16[128,5,7168]{2,0,1:T(8,128)(2,1)}) %all-gather.4.cloned.1.call-update) | async-done | bytes 9175056 | tf_op jit(solution)/shard_map/all_gather | solution.py:140
  401.3 14.0 %copy.85 = bf16[128,5,7168]{2,1,0:T(8,128)(2,1)} copy(bf16[128,5,7168]{2,0,1:T(8,128)(2,1)} %all-gather.4.cloned.1.call-done) | data formatting | bytes 18350080 | tf_op jit(solution)/shard_map/all_gather | solution.py:140
  415.3 15.1 %reshape.206 = bf16[640,7168]{1,0:T(8,128)(2,1)} reshape(bf16[128,5,7168]{2,1,0:T(8,128)(2,1)} %copy.85) | data formatting | bytes 18350080 | tf_op jit(solution)/shard_map/reshape | solution.py:141
  430.4 7.2 %fusion.8 = f32[640,256]{1,0:T(8,128)S(1)} fusion(bf16[640,7168]{1,0:T(8,128)(2,1)} %reshape.206, bf16[1,7168,256]{2,1,0:T(8,128)(2,1)} %param.31), kind=kOutput, calls=%fused_computation.16 | convolution fusion | flops 2348810240 | bytes 13500416 | tf_op jit(solution)/shard_map/dot_general | solution.py:143
  437.6 18.9 %convolution_convert_fusion = bf16[640,7168]{1,0:T(8,128)(2,1)} fusion(bf16[1,256,7168]{2,1,0:T(8,128)(2,1)} %param.33, bf16[640,7168]{1,0:T(8,128)(2,1)} %reshape.206, bf16[1,7168,256]{2,1,0:T(8,128)(2,1)} %param.32, f32[640,256]{1,0:T(8,128)S(1)} %fusion.8), kind=kOutput, calls=%fused_computation.1 | convolution fusion | flops 4703191040 | bytes 26345472 | tf_op jit(solution)/shard_map/dot_general | solution.py:147
  456.5 0.6 copy-done.13
  457.2 0.5 fusion.86
  457.7 1.3 iota_compare_fusion.4
  459.1 0.1 slice_bitcast_fusion.1
  459.1 4.9 select_select_fusion
  464.1 7.2 %all-to-all-start = ((bf16[16,2,256,576]{2,3,1,0:T(8,128)(2,1)}), bf16[16,2,256,576]{2,3,1,0:T(8,128)(2,1)}, u32[]{:S(2)}, u32[]{:S(2)}) async-start(bf16[16,2,256,576]{2,3,1,0:T(8,128)(2,1)} %select_select_fusion), calls=%async_computation | async-start | bytes 18874368 | tf_op jit(solution)/shard_map/all_to_all | solution.py:75
  471.2 0.1 fusion.84
  471.4 0.1 copy.76
  471.5 0.1 compare_reduce_fusion
  471.6 0.7 select_reduce_fusion.4
  477.3 0.1 reshape.209
  479.9 0.1 reduce_sum.116
  480.0 0.6 fusion.85
  480.6 1.4 pad_add_fusion
  482.1 0.2 fusion.66
  482.3 2.2 fusion.88
  484.6 0.3 fusion.38
  485.1 0.2 fusion.68
  485.3 1.6 add_convert_fusion
  486.9 148.7 %all-to-all-done = bf16[16,2,256,576]{2,3,1,0:T(8,128)(2,1)} async-done(((bf16[16,2,256,576]{2,3,1,0:T(8,128)(2,1)}), bf16[16,2,256,576]{2,3,1,0:T(8,128)(2,1)}, u32[]{:S(2)}, u32[]{:S(2)}) %all-to-all-start) | async-done | bytes 9437216 | tf_op jit(solution)/shard_map/all_to_all | solution.py:75
  635.6 1.3 dynamic-slice_bitcast_fusion
  637.0 1.1 fusion.87
  638.1 2.6 reshape.207
  640.7 10.5 %all-to-all-start.4 = ((bf16[16,5,7168]{2,1,0:T(8,128)(2,1)}), bf16[16,5,7168]{2,1,0:T(8,128)(2,1)S(1)}, u32[]{:S(2)}, u32[]{:S(2)}) async-start(bf16[16,5,7168]{2,1,0:T(8,128)(2,1)} %reshape.207), calls=%async_computation.6 | async-start | bytes 3670016 | tf_op jit(solution)/shard_map/all_to_all | solution.py:153
  651.2 0.1 pad_maximum_fusion
  651.3 1.1 copy.86
  652.4 0.1 fusion.57
  652.6 0.5 fusion.28
  653.1 1.1 pad_maximum_fusion.1
  654.1 23.0 %all-to-all-done.4 = bf16[16,5,7168]{2,1,0:T(8,128)(2,1)S(1)} async-done(((bf16[16,5,7168]{2,1,0:T(8,128)(2,1)}), bf16[16,5,7168]{2,1,0:T(8,128)(2,1)S(1)}, u32[]{:S(2)}, u32[]{:S(2)}) %all-to-all-start.4) | async-done | bytes 1146912 | tf_op jit(solution)/shard_map/all_to_all | solution.py:153
  677.1 0.6 reshape.208
  677.7 2.1 gather_fusion
  679.7 1.6 fusion.31
  681.4 0.7 fusion.56
  (69 shorter events, 0.9 us)
Async XLA Ops:
  7.2 138.6 %copy-start = (bf16[896,1152]{1,0:T(8,128)(2,1)S(1)}, bf16[896,1152]{1,0:T(8,128)(2,1)}, u32[]{:S(2)}) copy-start(bf16[896,1152]{1,0:T(8,128)(2,1)} %param.28) | copy-start | bytes 6193156
  7.2 50.6 %all-gather.6.cloned.1.call-start = ((), (), s32[]{:S(2)}) async-start(), calls=%async_computation.10 | async-start | bytes 1949696 | tf_op jit(solution)/shard_map/all_gather | solution.py:100
  10.1 215.8 %all-reduce.3.cloned.1.call-start = ((), (), s32[]{:S(2)}) async-start(), calls=%async_computation.11 | async-start | bytes 9437184 | tf_op jit(solution)/shard_map/psum | solution.py:107
  145.7 4.1 copy-start.16
  154.0 154.8 %reduce-scatter.3.cloned.1.call-start = ((), (), s32[]{:S(2)}) async-start(), calls=%async_computation.7 | async-start | bytes 1949696 | tf_op jit(solution)/shard_map/reduce_scatter | solution.py:111
  225.9 7.4 %copy-start.10 = (s32[8,8]{1,0:T(8,128)S(1)}, s32[8,8]{1,0:T(8,128)}, u32[]{:S(2)}) copy-start(s32[8,8]{1,0:T(8,128)} %param.34) | copy-start | bytes 772
  233.2 85.7 %copy-start.4 = (bf16[8,7168]{1,0:T(8,128)(2,1)S(1)}, bf16[8,7168]{1,0:T(8,128)(2,1)}, u32[]{:S(2)}) copy-start(bf16[8,7168]{1,0:T(8,128)(2,1)} %param.25) | copy-start | bytes 344068
  233.2 85.9 %copy-start.11 = (f32[7168]{0:T(1024)S(1)}, f32[7168]{0:T(1024)}, u32[]{:S(2)}) copy-start(f32[7168]{0:T(1024)} %param.30) | copy-start | bytes 86020
  308.7 10.2 %all-to-all-start.2 = ((bf16[8,8,896]{2,1,0:T(8,128)(2,1)}), bf16[8,8,896]{2,1,0:T(8,128)(2,1)S(1)}, u32[]{:S(2)}, u32[]{:S(2)}) async-start(bf16[8,8,896]{2,1,0:T(8,128)(2,1)} %bitcast.101), calls=%async_computation.3 | async-start | bytes 229376 | tf_op jit(solution)/shard_map/all_to_all | solution.py:117
  313.0 88.3 %all-gather.4.cloned.1.call-start = ((), (), s32[]{:S(2)}) async-start(), calls=%async_computation.8 | async-start | bytes 10321920 | tf_op jit(solution)/shard_map/all_gather | solution.py:140
  351.9 286.2 %reduce-scatter.5.cloned.1.call-start = ((), (), s32[]{:S(2)}) async-start(), calls=%async_computation.9 | async-start | bytes 10321920 | tf_op jit(solution)/shard_map/reduce_scatter | solution.py:146
  456.5 0.7 copy-start.13
  456.5 2.6 copy-start.3
  464.0 15.9 %copy-start.12 = (f32[8,8]{1,0:T(8,128)S(1)}, f32[8,8]{1,0:T(8,128)}, u32[]{:S(2)}) copy-start(f32[8,8]{1,0:T(8,128)} %param.35) | copy-start | bytes 772
  464.0 16.0 %copy-start.14 = (s32[128,2]{0,1:T(2,128)S(1)}, s32[128,2]{0,1:T(2,128)}, u32[]{:S(2)}) copy-start(s32[128,2]{0,1:T(2,128)} %param.23) | copy-start | bytes 3076
  464.0 18.0 %copy-start.15 = (s32[6]{0:T(128)S(1)}, s32[6]{0:T(128)}, u32[]{:S(2)}) copy-start(s32[6]{0:T(128)} %param.22) | copy-start | bytes 76
  464.0 18.1 %copy-start.9 = (bf16[8,576]{1,0:T(8,128)(2,1)S(1)}, bf16[8,576]{1,0:T(8,128)(2,1)}, u32[]{:S(2)}) copy-start(bf16[8,576]{1,0:T(8,128)(2,1)} %param.19) | copy-start | bytes 27652
  464.1 18.1 %copy-start.2 = (bf16[8,128,576]{1,2,0:T(8,128)(2,1)S(1)}, bf16[8,128,576]{1,2,0:T(8,128)(2,1)}, u32[]{:S(2)}) copy-start(bf16[8,128,576]{1,2,0:T(8,128)(2,1)} %param.18) | copy-start | bytes 3538948
  464.1 171.5 %all-to-all-start = ((bf16[16,2,256,576]{2,3,1,0:T(8,128)(2,1)}), bf16[16,2,256,576]{2,3,1,0:T(8,128)(2,1)}, u32[]{:S(2)}, u32[]{:S(2)}) async-start(bf16[16,2,256,576]{2,3,1,0:T(8,128)(2,1)} %select_select_fusion), calls=%async_computation | async-start | bytes 18874368 | tf_op jit(solution)/shard_map/all_to_all | solution.py:75
  482.3 2.9 copy-start.17
  637.0 3.7 copy-start.6
  640.7 36.4 %all-to-all-start.4 = ((bf16[16,5,7168]{2,1,0:T(8,128)(2,1)}), bf16[16,5,7168]{2,1,0:T(8,128)(2,1)S(1)}, u32[]{:S(2)}, u32[]{:S(2)}) async-start(bf16[16,5,7168]{2,1,0:T(8,128)(2,1)} %reshape.207), calls=%async_computation.6 | async-start | bytes 3670016 | tf_op jit(solution)/shard_map/all_to_all | solution.py:153
  651.2 1.2 copy-start.8
  651.2 1.4 copy-start.7
  651.3 1.8 copy-start.5
  677.7 4.4 copy-start.1
Sparse Core Ops, SparseCore 0:
  10.7 47.0 all-gather.5
  154.1 71.7 all-reduce.2
  233.4 75.3 reduce-scatter.2
  352.1 49.2 all-gather.3
  456.6 56.3 reduce-scatter.4
where the time goes:
time: 690 us; the launch traced here: 689 us
  waiting for transfers between devices  421 us (61%)
  local copies, waits for them, and re-layouts  100 us (14%)
  blocking collectives  58.7 us (9%)
  matrix products  49.5 us (7%)
  starting transfers between devices  22.3 us (3%)
  between operations  21.7 us (3%)
  other arithmetic  14.9 us (2%)
    all_to_all x1, waiting for transfers between devices, on_device(): lax.all_to_all(outgoing, 'tp', split_axis=0, concat_axis=0, tiled=True)  149 us
    reduce_scatter x1, waiting for transfers between devices, on_device(): lax.psum_scatter(jnp.dot(block, w_down, preferred_element_type=jnp.float3...  75.1 us
    psum x1, waiting for transfers between devices, on_device(): lax.psum(up_part.astype(jnp.bfloat16), 'dp').astype(jnp.float32)  71.9 us
    all_gather x1, waiting for transfers between devices, on_device(): pooled = lax.all_gather(received, 'dp', axis=0, tiled=True)  49.3 us
    all_gather x1, waiting for transfers between devices, on_device(): nearby = lax.all_gather(normed[None], 'tp', axis=0, tiled=True)  47.7 us
    unnamed x40, local copies, waits for them, and re-layouts  32.9 us
    all_to_all x1, blocking collectives, on_device(): lax.all_to_all(outgoing_rows, 'tp', split_axis=0, concat_axis=0, tiled=True)  29.9 us
    all_to_all x1, blocking collectives, on_device(): lax.all_to_all(nearby[:, None], 'dp', split_axis=3, concat_axis=1, tiled=...  28.8 us
  transfers between devices with their start and end apart: 8, of which 7 were waited for; matrix products, arithmetic and copies ran while one was open for 3% of the time, Pallas kernels for 0%

commit v1 on v0

--- a/solution.py
+++ b/solution.py
@@ -102,9 +102,15 @@
     features = gathered.reshape(-1, gathered.shape[-1])
     gate_part = jnp.dot(features, w_gate, preferred_element_type=jnp.float32)
     up_part = jnp.dot(features, w_up, preferred_element_type=jnp.float32)
+
+    def clear_the_plane(mat, axis_name):
+        block_now = lax.all_gather(mat, axis_name)
+        carry = jnp.sum(block_now, axis=0)
+        return carry
+
     gate, up = (
         lax.psum(gate_part.astype(jnp.bfloat16), "dp").astype(jnp.float32),
-        lax.psum(up_part.astype(jnp.bfloat16), "dp").astype(jnp.float32),
+        clear_the_plane(up_part.astype(jnp.bfloat16), "dp").astype(jnp.float32),
     )
     hidden_all = (jax.nn.silu(gate) * up).astype(jnp.bfloat16)
     block = hidden_all

time: 690 us -> 776 us (1.12)
  waiting for transfers between devices: 421 us -> 491 us
  other arithmetic: 14.9 us -> 26.7 us
    all_gather x0 -> x1, waiting for transfers between devices: none -> 83.8 us  [clear_the_plane(): block_now = lax.all_gather(mat, axis_name)]
    psum x1, waiting for transfers between devices: 71.9 us -> 57.7 us  [on_device(): lax.psum(gate_part.astype(jnp.bfloat16), 'dp').astype(jnp.float32)]
    reduce_sum x0 -> x1, other arithmetic: none -> 11.9 us  [clear_the_plane(): carry = jnp.sum(block_now, axis=0)]
    unnamed x40 -> x42, local copies, waits for them, and re-layouts: 32.9 us -> 35.6 us
  transfers between devices with their start and end apart: 8 -> 9, of which waited for: 7 -> 8; matrix products, arithmetic and copies ran while one was open for 3% -> 5% of each run, Pallas kernels for 0% -> 0%
where the time goes in v1:
time: 776 us; the launch traced here: 774 us
  waiting for transfers between devices  491 us (63%)
  local copies, waits for them, and re-layouts  103 us (13%)
  blocking collectives  58.7 us (8%)
  matrix products  51.1 us (7%)
  other arithmetic  26.7 us (3%)
  starting transfers between devices  22.3 us (3%)
  between operations  22 us (3%)
    all_to_all x1, waiting for transfers between devices, on_device(): lax.all_to_all(outgoing, 'tp', split_axis=0, concat_axis=0, tiled=True)  149 us
    all_gather x1, waiting for transfers between devices, clear_the_plane(): block_now = lax.all_gather(mat, axis_name)  83.8 us
    reduce_scatter x1, waiting for transfers between devices, on_device(): lax.psum_scatter(jnp.dot(block, w_down, preferred_element_type=jnp.float3...  74.4 us
    psum x1, waiting for transfers between devices, on_device(): lax.psum(gate_part.astype(jnp.bfloat16), 'dp').astype(jnp.float32)  57.7 us
    all_gather x1, waiting for transfers between devices, on_device(): pooled = lax.all_gather(received, 'dp', axis=0, tiled=True)  49.3 us
    all_gather x1, waiting for transfers between devices, on_device(): nearby = lax.all_gather(normed[None], 'tp', axis=0, tiled=True)  47.7 us
    unnamed x42, local copies, waits for them, and re-layouts  35.6 us
    all_to_all x1, blocking collectives, on_device(): lax.all_to_all(outgoing_rows, 'tp', split_axis=0, concat_axis=0, tiled=True)  29.9 us
  transfers between devices with their start and end apart: 9, of which 8 were waited for; matrix products, arithmetic and copies ran while one was open for 5% of the time, Pallas kernels for 0%

profile of v1, /device:TPU:0, one launch (start us, length us, event | category | flops | bytes accessed | tf_op | source)
XLA Modules:
  0.0 774.3 jit_solution(12230703137019717061)
XLA Ops:
  7.2 1.2 fusion.49
  8.4 1.6 fusion.51
  10.2 47.7 %all-gather.8.cloned.1.call-done = bf16[128,7168]{1,0:T(8,128)(2,1)} async-done(((bf16[8,7168]{1,0:T(8,128)(2,1)}), bf16[128,7168]{1,0:T(8,128)(2,1)}) %all-gather.8.cloned.1.call-update) | async-done | bytes 1835024 | tf_op jit(solution)/shard_map/all_gather | solution.py:100
  57.8 13.7 %copy.81 = bf16[16,1,8,7168]{0,2,1,3:T(8,128)(2,1)} copy(bf16[16,1,8,7168]{3,2,0,1:T(8,128)(2,1)} %bitcast.101) | data formatting | bytes 3670016 | tf_op jit(solution)/shard_map/broadcast_in_dim | solution.py:101
  71.6 17.3 %reshape.232 = bf16[8,2,57344]{2,1,0:T(2,128)(2,1)} reshape(bf16[7168,1,8,16]{3,2,1,0:T(8,128)(2,1)} %bitcast.95) | data formatting | bytes 3670016
  88.8 28.8 %all_to_all.39 = bf16[8,2,57344]{2,1,0:T(2,128)(2,1)} all-to-all(bf16[8,2,57344]{2,1,0:T(2,128)(2,1)} %reshape.232), channel_id=1, replica_groups=mesh['dp'=8,'tp'=16] {'dp'}, dimensions={0} | all-to-all | bytes 3670016 | tf_op jit(solution)/shard_map/all_to_all | solution.py:101
  117.6 12.5 %reshape.233 = bf16[7168,1,8,16]{3,2,1,0:T(8,128)(2,1)} reshape(bf16[8,2,57344]{2,1,0:T(2,128)(2,1)} %all_to_all.39) | data formatting | bytes 3670016
  130.1 13.8 %copy.95 = bf16[16,1,8,8,896]{4,3,2,0,1:T(8,128)(2,1)} copy(bf16[16,1,8,8,896]{0,2,4,3,1:T(8,128)(2,1)} %bitcast.96) | data formatting | bytes 3670016 | tf_op jit(solution)/shard_map/all_to_all | solution.py:101
  143.9 1.8 copy.83
  145.7 1.2 copy-done.3
  147.0 4.1 convolution_convert_fusion.2
  151.1 1.4 copy-done.4
  152.6 5.7 convolution_convert_fusion.3
  158.3 0.2 reduce-scatter.3.cloned.1.call-start
  158.5 83.8 %all-gather.10.cloned.1.call-done = bf16[8192,1152]{1,0:T(8,128)(2,1)} async-done(((bf16[1024,1152]{1,0:T(8,128)(2,1)}), bf16[8192,1152]{1,0:T(8,128)(2,1)}) %all-gather.10.cloned.1.call-update) | async-done | bytes 18874384 | tf_op jit(solution)/shard_map/all_gather | solution.py:107
  242.3 11.9 %reduce_sum.128 = bf16[1024,1152]{1,0:T(8,128)(2,1)} reduce(bf16[8,1024,1152]{2,1,0:T(8,128)(2,1)} %bitcast.97, bf16[]{:T(256)} %constant.130.clone.1), dimensions={0}, to_apply=%region_13.14 | reduce | flops 8257536 | bytes 21233666 | tf_op jit(solution)/shard_map/reduce_sum | solution.py:108
  254.2 57.7 %all-reduce.2.cloned.1.call-done = bf16[1024,1152]{1,0:T(8,128)(2,1)} async-done(((bf16[1024,1152]{1,0:T(8,128)(2,1)}), bf16[1024,1152]{1,0:T(8,128)(2,1)}) %all-reduce.2.cloned.1.call-update) | async-done | bytes 2359312 | tf_op jit(solution)/shard_map/psum | solution.py:112
  311.9 7.3 fusion.12
  319.4 0.3 select_reduce_fusion
  319.7 74.4 %reduce-scatter.3.cloned.1.call-done = bf16[64,896]{1,0:T(8,128)(2,1)} async-done(((bf16[1024,896]{1,0:T(8,128)(2,1)}), bf16[64,896]{1,0:T(8,128)(2,1)}) %reduce-scatter.3.cloned.1.call-update) | async-done | bytes 114704 | tf_op jit(solution)/shard_map/reduce_scatter | solution.py:117
  394.1 4.3 all-to-all-start.2
  398.4 0.1 fusion.65
  398.5 5.8 all-to-all-done.2
  404.4 0.2 fusion.53
  404.5 0.5 convolution_convert_fusion.1
  405.1 0.6 reshape.205
  405.6 29.9 %all_to_all.40 = bf16[16,5,7168]{2,1,0:T(8,128)(2,1)S(1)} all-to-all(bf16[16,5,7168]{2,1,0:T(8,128)(2,1)S(1)} %reshape.205), channel_id=1, replica_groups=mesh['dp'=8,'tp'=16] {'tp'}, dimensions={0} | all-to-all | bytes 2293760 | tf_op jit(solution)/shard_map/all_to_all | solution.py:145
  435.6 1.8 copy.84
  437.4 49.3 %all-gather.6.cloned.1.call-done = bf16[128,5,7168]{2,0,1:T(8,128)(2,1)} async-done(((bf16[16,5,7168]{2,0,1:T(8,128)(2,1)}), bf16[128,5,7168]{2,0,1:T(8,128)(2,1)}) %all-gather.6.cloned.1.call-update) | async-done | bytes 9175056 | tf_op jit(solution)/shard_map/all_gather | solution.py:146
  486.7 14.0 %copy.85 = bf16[128,5,7168]{2,1,0:T(8,128)(2,1)} copy(bf16[128,5,7168]{2,0,1:T(8,128)(2,1)} %all-gather.6.cloned.1.call-done) | data formatting | bytes 18350080 | tf_op jit(solution)/shard_map/all_gather | solution.py:146
  500.7 15.1 %reshape.206 = bf16[640,7168]{1,0:T(8,128)(2,1)} reshape(bf16[128,5,7168]{2,1,0:T(8,128)(2,1)} %copy.85) | data formatting | bytes 18350080 | tf_op jit(solution)/shard_map/reshape | solution.py:147
  515.8 7.2 fusion.8
  523.0 18.9 %convolution_convert_fusion = bf16[640,7168]{1,0:T(8,128)(2,1)} fusion(bf16[1,256,7168]{2,1,0:T(8,128)(2,1)} %param.33, bf16[640,7168]{1,0:T(8,128)(2,1)} %reshape.206, bf16[1,7168,256]{2,1,0:T(8,128)(2,1)} %param.32, f32[640,256]{1,0:T(8,128)S(1)} %fusion.8), kind=kOutput, calls=%fused_computation.1 | convolution fusion | flops 4703191040 | bytes 26345472 | tf_op jit(solution)/shard_map/dot_general | solution.py:153
  541.9 0.6 copy-done.15
  542.6 0.5 fusion.86
  543.1 1.3 iota_compare_fusion.4
  544.5 4.9 select_select_fusion
  549.5 7.2 all-to-all-start
  556.7 0.1 fusion.84
  556.9 0.1 compare_reduce_fusion
  557.0 0.7 select_reduce_fusion.4
  565.3 0.1 reduce_sum.129
  565.5 0.6 fusion.85
  566.0 1.4 pad_add_fusion
  567.5 0.2 fusion.66
  567.8 2.2 fusion.88
  570.0 0.3 fusion.38
  570.5 0.2 fusion.68
  570.7 1.6 add_convert_fusion
  572.3 148.7 %all-to-all-done = bf16[16,2,256,576]{2,3,1,0:T(8,128)(2,1)} async-done(((bf16[16,2,256,576]{2,3,1,0:T(8,128)(2,1)}), bf16[16,2,256,576]{2,3,1,0:T(8,128)(2,1)}, u32[]{:S(2)}, u32[]{:S(2)}) %all-to-all-start) | async-done | bytes 9437216 | tf_op jit(solution)/shard_map/all_to_all | solution.py:75
  721.0 1.3 dynamic-slice_bitcast_fusion
  722.4 1.1 fusion.87
  723.5 2.6 reshape.207
  726.1 10.5 %all-to-all-start.4 = ((bf16[16,5,7168]{2,1,0:T(8,128)(2,1)}), bf16[16,5,7168]{2,1,0:T(8,128)(2,1)S(1)}, u32[]{:S(2)}, u32[]{:S(2)}) async-start(bf16[16,5,7168]{2,1,0:T(8,128)(2,1)} %reshape.207), calls=%async_computation.6 | async-start | bytes 3670016 | tf_op jit(solution)/shard_map/all_to_all | solution.py:159
  736.6 0.1 pad_maximum_fusion
  736.7 1.1 copy.86
  737.8 0.1 fusion.57
  738.0 0.5 fusion.28
  738.5 1.1 pad_maximum_fusion.1
  739.5 23.0 %all-to-all-done.4 = bf16[16,5,7168]{2,1,0:T(8,128)(2,1)S(1)} async-done(((bf16[16,5,7168]{2,1,0:T(8,128)(2,1)}), bf16[16,5,7168]{2,1,0:T(8,128)(2,1)S(1)}, u32[]{:S(2)}, u32[]{:S(2)}) %all-to-all-start.4) | async-done | bytes 1146912 | tf_op jit(solution)/shard_map/all_to_all | solution.py:159
  762.5 0.6 reshape.208
  763.1 2.1 gather_fusion
  765.1 1.6 fusion.31
  766.8 0.7 fusion.56
  (75 shorter events, 1.3 us)
Async XLA Ops:
  7.2 139.8 %copy-start = (bf16[896,1152]{1,0:T(8,128)(2,1)S(1)}, bf16[896,1152]{1,0:T(8,128)(2,1)}, u32[]{:S(2)}) copy-start(bf16[896,1152]{1,0:T(8,128)(2,1)} %param.28) | copy-start | bytes 6193156
  7.2 50.6 %all-gather.8.cloned.1.call-start = ((), (), s32[]{:S(2)}) async-start(), calls=%async_computation.11 | async-start | bytes 1949696 | tf_op jit(solution)/shard_map/all_gather | solution.py:100
  10.1 232.2 %all-gather.10.cloned.1.call-start = ((), (), s32[]{:S(2)}) async-start(), calls=%async_computation.12 | async-start | bytes 21233664 | tf_op jit(solution)/shard_map/all_gather | solution.py:107
  145.7 1.3 copy-start.3
  151.1 1.5 copy-start.4
  151.1 160.8 %all-reduce.2.cloned.1.call-start = ((), (), s32[]{:S(2)}) async-start(), calls=%async_computation.7 | async-start | bytes 4718592 | tf_op jit(solution)/shard_map/psum | solution.py:112
  158.3 235.9 %reduce-scatter.3.cloned.1.call-start = ((), (), s32[]{:S(2)}) async-start(), calls=%async_computation.8 | async-start | bytes 1949696 | tf_op jit(solution)/shard_map/reduce_scatter | solution.py:117
  254.2 65.1 %copy-start.12 = (s32[8,8]{1,0:T(8,128)S(1)}, s32[8,8]{1,0:T(8,128)}, u32[]{:S(2)}) copy-start(s32[8,8]{1,0:T(8,128)} %param.34) | copy-start | bytes 772
  319.2 85.1 %copy-start.6 = (bf16[8,7168]{1,0:T(8,128)(2,1)S(1)}, bf16[8,7168]{1,0:T(8,128)(2,1)}, u32[]{:S(2)}) copy-start(bf16[8,7168]{1,0:T(8,128)(2,1)} %param.25) | copy-start | bytes 344068
  319.2 85.3 %copy-start.13 = (f32[7168]{0:T(1024)S(1)}, f32[7168]{0:T(1024)}, u32[]{:S(2)}) copy-start(f32[7168]{0:T(1024)} %param.30) | copy-start | bytes 86020
  394.1 10.2 %all-to-all-start.2 = ((bf16[8,8,896]{2,1,0:T(8,128)(2,1)}), bf16[8,8,896]{2,1,0:T(8,128)(2,1)S(1)}, u32[]{:S(2)}, u32[]{:S(2)}) async-start(bf16[8,8,896]{2,1,0:T(8,128)(2,1)} %bitcast.103), calls=%async_computation.3 | async-start | bytes 229376 | tf_op jit(solution)/shard_map/all_to_all | solution.py:123
  398.4 88.4 %all-gather.6.cloned.1.call-start = ((), (), s32[]{:S(2)}) async-start(), calls=%async_computation.9 | async-start | bytes 10321920 | tf_op jit(solution)/shard_map/all_gather | solution.py:146
  437.3 286.2 %reduce-scatter.5.cloned.1.call-start = ((), (), s32[]{:S(2)}) async-start(), calls=%async_computation.10 | async-start | bytes 10321920 | tf_op jit(solution)/shard_map/reduce_scatter | solution.py:152
  541.9 0.7 copy-start.15
  541.9 2.6 copy-start.5
  549.4 15.9 %copy-start.14 = (f32[8,8]{1,0:T(8,128)S(1)}, f32[8,8]{1,0:T(8,128)}, u32[]{:S(2)}) copy-start(f32[8,8]{1,0:T(8,128)} %param.35) | copy-start | bytes 772
  549.5 16.0 %copy-start.16 = (s32[128,2]{0,1:T(2,128)S(1)}, s32[128,2]{0,1:T(2,128)}, u32[]{:S(2)}) copy-start(s32[128,2]{0,1:T(2,128)} %param.23) | copy-start | bytes 3076
  549.5 18.0 %copy-start.17 = (s32[6]{0:T(128)S(1)}, s32[6]{0:T(128)}, u32[]{:S(2)}) copy-start(s32[6]{0:T(128)} %param.22) | copy-start | bytes 76
  549.5 18.1 %copy-start.11 = (bf16[8,576]{1,0:T(8,128)(2,1)S(1)}, bf16[8,576]{1,0:T(8,128)(2,1)}, u32[]{:S(2)}) copy-start(bf16[8,576]{1,0:T(8,128)(2,1)} %param.19) | copy-start | bytes 27652
  549.5 18.1 %copy-start.2 = (bf16[8,128,576]{1,2,0:T(8,128)(2,1)S(1)}, bf16[8,128,576]{1,2,0:T(8,128)(2,1)}, u32[]{:S(2)}) copy-start(bf16[8,128,576]{1,2,0:T(8,128)(2,1)} %param.18) | copy-start | bytes 3538948
  549.5 171.5 %all-to-all-start = ((bf16[16,2,256,576]{2,3,1,0:T(8,128)(2,1)}), bf16[16,2,256,576]{2,3,1,0:T(8,128)(2,1)}, u32[]{:S(2)}, u32[]{:S(2)}) async-start(bf16[16,2,256,576]{2,3,1,0:T(8,128)(2,1)} %select_select_fusion), calls=%async_computation | async-start | bytes 18874368 | tf_op jit(solution)/shard_map/all_to_all | solution.py:75
  567.8 2.9 copy-start.18
  722.4 3.7 copy-start.8
  726.1 36.4 %all-to-all-start.4 = ((bf16[16,5,7168]{2,1,0:T(8,128)(2,1)}), bf16[16,5,7168]{2,1,0:T(8,128)(2,1)S(1)}, u32[]{:S(2)}, u32[]{:S(2)}) async-start(bf16[16,5,7168]{2,1,0:T(8,128)(2,1)} %reshape.207), calls=%async_computation.6 | async-start | bytes 3670016 | tf_op jit(solution)/shard_map/all_to_all | solution.py:159
  736.6 1.2 copy-start.10
  736.6 1.4 copy-start.9
  736.7 1.8 copy-start.7
  763.1 4.4 copy-start.1
Sparse Core Ops, SparseCore 0:
  10.7 47.0 all-gather.7
  151.2 91.0 all-gather.9
  244.7 67.1 all-reduce.1
  319.4 74.7 reduce-scatter.2
  437.5 49.2 all-gather.5
  542.0 56.3 reduce-scatter.4
